TPU v7x, 256 devices: a whole 4x4x8 slice. The times are simulated.
256 devices in a mesh: row: 8 (over z_hi, core), col: 4 (over x), cfg: 8 (over y, z_lo).
Axes of the slice: x: 4, y: 4, z: 8 (z_hi: 4, z_lo: 2; z = z_hi * 2 + z_lo), core: 2. Of those that a mesh axis runs over, the one named last changes fastest.
Arguments:
- eigvec: bfloat16 [18432, 18432], P('row', ('col', 'cfg')), may hold values from -0.046875 to 0.046875
- force_const: bfloat16 [18432, 18432], P(('col', 'cfg'), 'row'), may hold values from -0.046875 to 0.046875
- amplitudes: bfloat16 [18432, 1024], P(('col', 'cfg')), may hold values from -6 to 6
- mlip_forces: bfloat16 [18432, 1024], P(('col', 'cfg'), 'row'), may hold values from -6 to 6
- frequency: float32 [18432], P(('col', 'cfg')), may hold values from 0.25 to 4
Outputs:
- gradient: float32 [18432, 18432], P(('col', 'cfg'), 'row')
All inputs are finite; a program needn't handle non-finite values.
Results may differ from a plain program's by a relative error of at most 0.0055.
Values may be sent and summed in bfloat16 or wider, within the bound.
A program may use at most 64 MiB of HBM per device.

v0:
```python
import jax
import jax.numpy as jnp
from jax import lax
from jax.sharding import PartitionSpec as P


def local(eigvec, force_const, amplitudes, mlip_forces, frequency):
    mode_scale = 1.0 / jnp.sqrt(2.0 * frequency)
    scaled_amp = (mode_scale[:, None] * amplitudes.astype(jnp.float32)).astype(jnp.bfloat16)
    own_rows = lax.psum_scatter(
        lax.dot_general(
            scaled_amp, eigvec, (((0,), (1,)), ((), ())), preferred_element_type=jnp.float32
        ),
        ("col", "cfg"),
        scatter_dimension=0,
        tiled=True,
    )
    displaced = lax.all_gather(own_rows.astype(jnp.bfloat16), ("col", "cfg"), axis=0, tiled=True)
    harmonic = lax.dot_general(
        force_const, displaced, (((1,), (1,)), ((), ())), preferred_element_type=jnp.float32
    )
    own_forces = lax.psum_scatter(harmonic, "row", scatter_dimension=1, tiled=True)
    own_resid = (mlip_forces.astype(jnp.float32) + own_forces).astype(jnp.bfloat16)
    residual = lax.all_gather(own_resid, "row", axis=1, tiled=True)
    total = jnp.dot(residual, displaced, preferred_element_type=jnp.float32)
    return total / jnp.sqrt(jnp.float32(displaced.shape[0]))


def solution(mesh):
    return jax.shard_map(
        local,
        mesh=mesh,
        in_specs=(
            P("row", ("col", "cfg")),
            P(("col", "cfg"), "row"),
            P(("col", "cfg"), None),
            P(("col", "cfg"), "row"),
            P(("col", "cfg")),
        ),
        out_specs=P(("col", "cfg"), "row"),
        check_vma=False,
    )
```

profile of v0, /device:TPU:1, one launch (start us, length us, event | category | flops | bytes accessed | tf_op | source)
XLA Modules:
  0.0 504.7 jit_solution(2931063429709226852)
XLA Ops:
  6.5 0.0 copy-start
  6.5 0.0 reduce-scatter.3.cloned.1.call-start
  6.5 0.8 multiply_rsqrt_fusion
  7.4 0.9 copy-done
  8.3 8.0 %fusion = f32[1024,2304]{1,0:T(8,128)} fusion(bf16[2304,576]{0,1:T(8,128)(2,1)S(1)} %copy-done, bf16[576,1024]{1,0:T(8,128)(2,1)} %param.7, f32[576]{0:T(1024)S(1)} %multiply_rsqrt_fusion), kind=kOutput, calls=%fused_computation.3 | convolution fusion | flops 2719678464 | bytes 13273344 | tf_op jit(solution)/shard_map/dot_general | solution.py:11
  16.3 0.0 reduce-scatter.3.cloned.1.call-update
  16.4 0.0 all-gather.3.cloned.1.call-start
  16.4 217.5 %reduce-scatter.3.cloned.1.call-done = f32[32,2304]{1,0:T(8,128)} async-done(((f32[1024,2304]{1,0:T(8,128)}), f32[32,2304]{1,0:T(8,128)}) %reduce-scatter.3.cloned.1.call-update) | async-done | bytes 294928 | tf_op jit(solution)/shard_map/reduce_scatter | solution.py:10
  233.9 1.6 convert_element_type.18
  235.5 0.0 all-gather.3.cloned.1.call-update
  235.6 0.0 copy-start.1
  235.6 0.0 reduce-scatter.5.cloned.1.call-start
  235.6 147.8 %all-gather.3.cloned.1.call-done = bf16[1024,2304]{1,0:T(8,128)(2,1)} async-done(((bf16[32,2304]{1,0:T(8,128)(2,1)}), bf16[1024,2304]{1,0:T(8,128)(2,1)}) %all-gather.3.cloned.1.call-update) | async-done | bytes 4718608 | tf_op jit(solution)/shard_map/all_gather | solution.py:18
  383.4 7.5 %convolution_bitcast_fusion = f32[576,1024]{1,0:T(8,128)} fusion(bf16[1024,2304]{1,0:T(8,128)(2,1)} %all-gather.3.cloned.1.call-done, bf16[576,2304]{1,0:T(8,128)(2,1)} %param.6), kind=kOutput, calls=%fused_computation.2 | convolution fusion | flops 2717908992 | bytes 9732096 | tf_op jit(solution)/shard_map/dot_general | solution.py:19
  390.9 0.0 reduce-scatter.5.cloned.1.call-update
  390.9 0.0 all-gather.5.cloned.1.call-start
  391.0 63.1 %reduce-scatter.5.cloned.1.call-done = f32[576,128]{1,0:T(8,128)} async-done(((f32[576,1024]{1,0:T(8,128)}), f32[576,128]{1,0:T(8,128)}) %reduce-scatter.5.cloned.1.call-update) | async-done | bytes 294928 | tf_op jit(solution)/shard_map/reduce_scatter | solution.py:22
  454.1 0.0 copy-done.1
  454.1 1.7 add_convert_fusion
  455.8 0.0 all-gather.5.cloned.1.call-update
  455.8 34.4 %all-gather.5.cloned.1.call-done = bf16[576,1024]{1,0:T(8,128)(2,1)} async-done(((bf16[576,128]{1,0:T(8,128)(2,1)}), bf16[576,1024]{1,0:T(8,128)(2,1)}) %all-gather.5.cloned.1.call-update) | async-done | bytes 1179664 | tf_op jit(solution)/shard_map/all_gather | solution.py:24
  490.2 8.0 %convolution_multiply_fusion = f32[576,2304]{1,0:T(8,128)} fusion(bf16[576,1024]{1,0:T(8,128)(2,1)} %all-gather.5.cloned.1.call-done, bf16[1024,2304]{1,0:T(8,128)(2,1)} %all-gather.3.cloned.1.call-done), kind=kOutput, calls=%fused_computation | convolution fusion | flops 2719236096 | bytes 11206656 | tf_op jit(solution)/shard_map/dot_general | solution.py:25
Async XLA Ops:
  6.5 1.8 copy-start
  6.5 227.4 %reduce-scatter.3.cloned.1.call-start = ((), (), s32[]{:S(2)}) async-start(), calls=%async_computation.2 | async-start | bytes 9732096 | tf_op jit(solution)/shard_map/reduce_scatter | solution.py:10
  16.4 367.0 %all-gather.3.cloned.1.call-start = ((), (), s32[]{:S(2)}) async-start(), calls=%async_computation.3 | async-start | bytes 4866048 | tf_op jit(solution)/shard_map/all_gather | solution.py:18
  235.6 218.6 %copy-start.1 = (bf16[576,128]{1,0:T(8,128)(2,1)S(1)}, bf16[576,128]{1,0:T(8,128)(2,1)}, u32[]{:S(2)}) copy-start(bf16[576,128]{1,0:T(8,128)(2,1)} %param.8) | copy-start | bytes 442372
  235.6 218.5 %reduce-scatter.5.cloned.1.call-start = ((), (), s32[]{:S(2)}) async-start(), calls=%async_computation.4 | async-start | bytes 2654208 | tf_op jit(solution)/shard_map/reduce_scatter | solution.py:22
  390.9 99.3 %all-gather.5.cloned.1.call-start = ((), (), s32[]{:S(2)}) async-start(), calls=%async_computation.5 | async-start | bytes 1327104 | tf_op jit(solution)/shard_map/all_gather | solution.py:24
Sparse Core Ops, SparseCore 0:
  16.5 217.3 reduce-scatter.2
  235.7 147.6 all-gather.2
  391.1 63.0 reduce-scatter.4
  455.9 34.2 all-gather.4
where the time goes:
time: 505 us
  waiting for transfers between devices  463 us (92%)
  matrix products  23.6 us (5%)
  between operations  13.1 us (3%)
    reduce_scatter x1, waiting for transfers between devices, local(): lax.psum_scatter(lax.dot_general(scaled_amp, eigvec, (((0,), (1,)), ((),...  217 us
    all_gather x1, waiting for transfers between devices, local(): lax.all_gather(own_rows.astype(jnp.bfloat16), ('col', 'cfg'), axis=0, til...  148 us
    reduce_scatter x1, waiting for transfers between devices, local(): lax.psum_scatter(harmonic, 'row', scatter_dimension=1, tiled=True)  63.1 us
    all_gather x1, waiting for transfers between devices, local(): residual = lax.all_gather(own_resid, 'row', axis=1, tiled=True)  34.4 us
  transfers between devices with their start and end apart: 4, of which 4 were waited for; matrix products, arithmetic and copies ran while one was open for 0% of the time, Pallas kernels for 0%

commit v1 on v0

v1 whole, which is shorter than its diff:
```python
import functools

import jax
import jax.numpy as jnp
from jax import lax
from jax.experimental import pallas as pl
from jax.experimental.pallas import tpu as pltpu
from jax.sharding import PartitionSpec as P

MESH = pl.DeviceIdType.MESH
PAIRS = 4
LANES = 128
ORDER = [(8, 2), (4, 1), (0, 0), (9, 2), (5, 1), (1, 0), (10, 2), (6, 1), (2, 0), (11, 2), (7, 1), (3, 0)]


def comm_kernel(
    eig_hbm, fc_hbm, amp_hbm, forces_hbm, freq_ref, resid_hbm, disp_hbm,
    eig, fc, amp, scale, part32, part16, in_opp, in_near, sum32, sum16, in_second, own32, own16, in_zl,
    disp, harm, in_core, harm32, harm16, in_zh, force_in, force_own, resid,
    load_sem, col_send, col_recv, row_send, row_recv, m_send, m_recv, out_sem,
):
    rows = eig_hbm.shape[0]
    quarter, sub = rows // 4, rows // 16
    half = quarter // 2
    out_rows = fc_hbm.shape[0]
    piece = out_rows // 4

    row, x, cfg = lax.axis_index("row"), lax.axis_index("col"), lax.axis_index("cfg")
    zh, core, y, zl = row // 2, row % 2, cfg // 2, cfg % 2

    def x_dev(d):
        return {"col": (x + d) % 4}

    def y_dev(d):
        return {"cfg": ((y + d) % 4) * 2 + zl}

    def zh_dev(d):
        return {"row": ((zh + d) % 4) * 2 + core}

    zl_dev = {"cfg": y * 2 + (1 - zl)}
    core_dev = {"row": zh * 2 + (1 - core)}
    axes = [(x, x_dev, y, y_dev), (y, y_dev, x, x_dev)]

    loads = [pltpu.make_async_copy(amp_hbm.at[:, pl.ds(p * 2 * LANES, 2 * LANES)], amp.at[p], load_sem.at[p]) for p in range(PAIRS)]
    loads += [pltpu.make_async_copy(eig_hbm.at[pl.ds(q * quarter, quarter)], eig.at[q], load_sem.at[4 + q]) for q in range(4)]
    load_fc = pltpu.make_async_copy(fc_hbm, fc, load_sem.at[8])
    load_forces = [pltpu.make_async_copy(forces_hbm.at[pl.ds(q * piece, piece)], force_own.at[q], load_sem.at[9 + q]) for q in range(4)]
    for c in loads:
        c.start()
    for c in load_forces:
        c.start()
    load_fc.start()

    barrier = pltpu.get_barrier_semaphore()
    peers = [x_dev(1), x_dev(2), x_dev(3), y_dev(1), y_dev(2), y_dev(3), zh_dev(1), zh_dev(2), zh_dev(3), zl_dev, core_dev]
    for dev in peers:
        pl.semaphore_signal(barrier, inc=1, device_id=dev, device_id_type=MESH)

    modes = scale.shape[0]
    f = freq_ref[...].reshape(1, modes)
    on_diag = lax.broadcasted_iota(jnp.int32, (modes, modes), 0) == lax.broadcasted_iota(jnp.int32, (modes, modes), 1)
    f_col = jnp.sum(jnp.where(on_diag, f, 0.0), axis=1, keepdims=True)
    scale[...] = jnp.broadcast_to(1.0 / jnp.sqrt(2.0 * f_col), scale.shape)

    for c in loads:
        c.wait()
    for c in load_forces:
        c.wait()

    def col_copy(p, t, k, src, dst, dev):
        return pltpu.make_async_remote_copy(
            src_ref=src, dst_ref=dst, send_sem=col_send.at[p, t, k], recv_sem=col_recv.at[p, t, k],
            device_id=dev, device_id_type=MESH,
        )

    def row_copy(p, k, src, dst, dev):
        return pltpu.make_async_remote_copy(
            src_ref=src, dst_ref=dst, send_sem=row_send.at[p, k], recv_sem=row_recv.at[p, k],
            device_id=dev, device_id_type=MESH,
        )

    lo, hi = pl.ds(0, half), pl.ds(half, half)

    def first_out(p, t, k):
        a, a_dev, _, _ = axes[t]
        q1, q2, q3 = (a + 1) % 4, (a + 2) % 4, (a + 3) % 4
        src, dst, dev = [
            (part16.at[p, t, q2, lo], in_opp.at[p, t, 0], 1),
            (part16.at[p, t, q2, hi], in_opp.at[p, t, 1], 3),
            (part16.at[p, t, q1, hi], in_near.at[p, t, 0, hi], 1),
            (part16.at[p, t, q3, lo], in_near.at[p, t, 1, lo], 3),
            (part16.at[p, t, q1, lo], in_near.at[p, t, 0, lo], 1),
            (part16.at[p, t, q3, hi], in_near.at[p, t, 1, hi], 3),
        ][k]
        return col_copy(p, t, k, src, dst, a_dev(dev))

    def second_out(p, t, d):
        _, _, b, b_dev = axes[t]
        return col_copy(p, t, 5 + d, sum16.at[p, t, (b + d) % 4], in_second.at[p, t, d - 1], b_dev(d))

    def zl_out(p, t):
        return col_copy(p, t, 9, own16.at[p, t], in_zl.at[p, t], zl_dev)

    def disp_at(p, t, start, size, align):
        return disp.at[p, pl.ds(pl.multiple_of(start, align), size), pl.ds(t * LANES, LANES)]

    def spread_b(p, t, d, owner):
        a, _, _, b_dev = axes[t]
        at = disp_at(p, t, a * quarter + owner * sub, sub, 16)
        return col_copy(p, t, 9 + d, at, at, b_dev(d))

    def spread_a(p, t, k, owner):
        _, a_dev, _, _ = axes[t]
        which, dev = [(0, 1), (1, 1), (1, 3), (0, 3), (0, 1), (1, 3)][k]
        at = disp_at(p, t, owner * quarter + which * half, half, 16)
        return col_copy(p, t, 13 + k, at, at, a_dev(dev))

    def core_out(p):
        return row_copy(p, 0, harm.at[p, 1 - core], in_core.at[p], core_dev)

    def zh_out(p, d):
        return row_copy(p, d, harm16.at[p, (zh + d) % 4], in_zh.at[p, d - 1], zh_dev(d))

    def resid_spread(p, d, owner):
        at = resid.at[p, core, owner]
        return row_copy(p, 3 + d, at, at, zh_dev(d))

    def resid_core(p, which):
        at = resid.at[p, which]
        return row_copy(p, 7, at, at, core_dev)

    def force_out(d, slot):
        return pltpu.make_async_remote_copy(
            src_ref=force_own.at[(zh + d) % 4], dst_ref=force_in.at[slot],
            send_sem=m_send.at[d - 1], recv_sem=m_recv.at[d - 1], device_id=zh_dev(d), device_id_type=MESH,
        )

    def compute_part(p):
        scaled = (scale[:, :1] * amp[p].astype(jnp.float32)).astype(jnp.bfloat16)

        def one(q, carry):
            product = jnp.dot(eig[q], scaled, preferred_element_type=jnp.float32)
            for t in range(2):
                block = product[:, t * LANES : (t + 1) * LANES]
                part32[p, t, q] = block
                part16[p, t, q] = block.astype(jnp.bfloat16)
            return carry

        lax.fori_loop(0, 4, one, 0)

    def send_part(p):
        for k in range(4):
            for t in range(2):
                first_out(p, t, k).start()

    def stage0(p):
        @pl.when(p > 0)
        def _():
            compute_part(p)
            send_part(p)

    def stage1(p):
        for t in range(2):
            a = axes[t][0]
            first_out(p, t, 0).wait_recv()
            q1, q3 = (a + 1) % 4, (a + 3) % 4
            part16[p, t, q1, lo] = (part32[p, t, q1, lo] + in_opp[p, t, 0].astype(jnp.float32)).astype(jnp.bfloat16)
            first_out(p, t, 4).start()
            first_out(p, t, 1).wait_recv()
            part16[p, t, q3, hi] = (part32[p, t, q3, hi] + in_opp[p, t, 1].astype(jnp.float32)).astype(jnp.bfloat16)
            first_out(p, t, 5).start()

    def stage2(p):
        for t in range(2):
            a, _, b, _ = axes[t]
            for k in range(2, 6):
                first_out(p, t, k).wait_recv()
            total = part32[p, t, a] + in_near[p, t, 0].astype(jnp.float32) + in_near[p, t, 1].astype(jnp.float32)
            total = total.reshape(4, sub, LANES)
            sum32[p, t] = total
            sum16[p, t] = total.astype(jnp.bfloat16)
            for d in (2, 1, 3):
                second_out(p, t, d).start()

    def stage3(p):
        for t in range(2):
            b = axes[t][2]
            for d in (1, 2, 3):
                second_out(p, t, d).wait_recv()
            total = sum32[p, t, b]
            for d in range(3):
                total += in_second[p, t, d].astype(jnp.float32)
            own32[p, t] = total
            own16[p, t] = total.astype(jnp.bfloat16)
            zl_out(p, t).start()

    def stage4(p):
        for t in range(2):
            a, _, b, _ = axes[t]
            zl_out(p, t).wait_recv()
            value = (own32[p, t] + in_zl[p, t].astype(jnp.float32)).astype(jnp.bfloat16)
            disp[p, pl.ds(pl.multiple_of(a * quarter + b * sub, 16), sub), pl.ds(t * LANES, LANES)] = value
            for d in (2, 1, 3):
                spread_b(p, t, d, b).start()

    def stage5(p):
        for t in range(2):
            a, _, b, _ = axes[t]
            for d in (1, 2, 3):
                spread_b(p, t, d, (b + 4 - d) % 4).wait_recv()
            for k in (0, 2, 1, 3):
                spread_a(p, t, k, a).start()

    def stage6(p):
        for t in range(2):
            a = axes[t][0]
            below, above = (a + 3) % 4, (a + 1) % 4
            spread_a(p, t, 0, below).wait_recv()
            spread_a(p, t, 4, below).start()
            spread_a(p, t, 2, above).wait_recv()
            spread_a(p, t, 5, above).start()

    def stage7(p):
        for t in range(2):
            a = axes[t][0]
            below, above, far = (a + 3) % 4, (a + 1) % 4, (a + 2) % 4
            spread_a(p, t, 1, below).wait_recv()
            spread_a(p, t, 3, above).wait_recv()
            spread_a(p, t, 4, far).wait_recv()
            spread_a(p, t, 5, far).wait_recv()
        pltpu.make_async_copy(disp.at[p], disp_hbm.at[p], out_sem.at[p, 0]).start()

        @pl.when(p == 0)
        def _():
            load_fc.wait()
            for d in (1, 2, 3):
                force_out(d, (zh + 4 - d) % 4).wait_recv()

        product = jnp.dot(fc[...], disp[p], preferred_element_type=jnp.float32)
        for t in range(2):
            harm[p, t] = product[:, t * LANES : (t + 1) * LANES]
        core_out(p).start()

    def stage8(p):
        core_out(p).wait_recv()
        total = (harm[p, core] + in_core[p]).reshape(4, piece, LANES)
        harm32[p] = total
        harm16[p] = total.astype(jnp.bfloat16)
        for d in (2, 1, 3):
            zh_out(p, d).start()

    def stage9(p):
        for d in (1, 2, 3):
            zh_out(p, d).wait_recv()
        total = force_in[p].astype(jnp.float32) + harm32[p, zh]
        for d in range(3):
            total += in_zh[p, d].astype(jnp.float32)
        resid[p, core, zh] = total.astype(jnp.bfloat16)
        for d in (2, 1, 3):
            resid_spread(p, d, zh).start()

    def stage10(p):
        for d in (1, 2, 3):
            resid_spread(p, d, (zh + 4 - d) % 4).wait_recv()
        resid_core(p, core).start()

    def stage11(p):
        resid_core(p, 1 - core).wait_recv()
        pltpu.make_async_copy(resid.at[p], resid_hbm.at[p], out_sem.at[p, 1]).start()

    stages = [stage0, stage1, stage2, stage3, stage4, stage5, stage6, stage7, stage8, stage9, stage10, stage11]

    compute_part(0)
    force_in[zh] = force_own[zh]
    pl.semaphore_wait(barrier, len(peers))
    send_part(0)
    for d in (1, 2, 3):
        force_out(d, zh).start()

    def turn(u, carry):
        for s, offset in ORDER:
            p = u - offset

            @pl.when((p >= 0) & (p < PAIRS))
            def _(s=s, p=p):
                stages[s](p)

        return carry

    lax.fori_loop(0, PAIRS + max(o for _, o in ORDER), turn, 0)

    def drain(p, carry):
        for t in range(2):
            a, _, b, _ = axes[t]
            for k in range(6):
                first_out(p, t, k).wait_send()
                spread_a(p, t, k, a).wait_send()
            for d in (1, 2, 3):
                second_out(p, t, d).wait_send()
                spread_b(p, t, d, b).wait_send()
            zl_out(p, t).wait_send()
        core_out(p).wait_send()
        for d in (1, 2, 3):
            zh_out(p, d).wait_send()
            resid_spread(p, d, zh).wait_send()
        resid_core(p, core).wait_send()
        pltpu.make_async_copy(disp.at[p], disp_hbm.at[p], out_sem.at[p, 0]).wait()
        pltpu.make_async_copy(resid.at[p], resid_hbm.at[p], out_sem.at[p, 1]).wait()
        return carry

    lax.fori_loop(0, PAIRS, drain, 0)
    for d in (1, 2, 3):
        force_out(d, zh).wait_send()


def exchange(eigvec, force_const, amplitudes, mlip_forces, frequency):
    rows, modes = eigvec.shape
    out_rows = force_const.shape[0]
    quarter, sub, piece = rows // 4, rows // 16, out_rows // 4
    half = quarter // 2
    bf16, f32 = jnp.bfloat16, jnp.float32
    anywhere = pl.BlockSpec(memory_space=pl.ANY)
    dma = pltpu.SemaphoreType.DMA
    return pl.pallas_call(
        comm_kernel,
        name="exchange",
        out_shape=[
            jax.ShapeDtypeStruct((PAIRS, 2, 4, piece, LANES), bf16),
            jax.ShapeDtypeStruct((PAIRS, rows, 2 * LANES), bf16),
        ],
        in_specs=[anywhere] * 4 + [pl.BlockSpec(memory_space=pltpu.VMEM)],
        out_specs=[anywhere, anywhere],
        scratch_shapes=[
            pltpu.VMEM((4, quarter, modes), bf16),
            pltpu.VMEM((out_rows, rows), bf16),
            pltpu.VMEM((PAIRS, modes, 2 * LANES), bf16),
            pltpu.VMEM((modes, LANES), f32),
            pltpu.VMEM((PAIRS, 2, 4, quarter, LANES), f32),
            pltpu.VMEM((PAIRS, 2, 4, quarter, LANES), bf16),
            pltpu.VMEM((PAIRS, 2, 2, half, LANES), bf16),
            pltpu.VMEM((PAIRS, 2, 2, quarter, LANES), bf16),
            pltpu.VMEM((PAIRS, 2, 4, sub, LANES), f32),
            pltpu.VMEM((PAIRS, 2, 4, sub, LANES), bf16),
            pltpu.VMEM((PAIRS, 2, 3, sub, LANES), bf16),
            pltpu.VMEM((PAIRS, 2, sub, LANES), f32),
            pltpu.VMEM((PAIRS, 2, sub, LANES), bf16),
            pltpu.VMEM((PAIRS, 2, sub, LANES), bf16),
            pltpu.VMEM((PAIRS, rows, 2 * LANES), bf16),
            pltpu.VMEM((PAIRS, 2, out_rows, LANES), f32),
            pltpu.VMEM((PAIRS, out_rows, LANES), f32),
            pltpu.VMEM((PAIRS, 4, piece, LANES), f32),
            pltpu.VMEM((PAIRS, 4, piece, LANES), bf16),
            pltpu.VMEM((PAIRS, 3, piece, LANES), bf16),
            pltpu.VMEM((PAIRS, piece, LANES), bf16),
            pltpu.VMEM((4, piece, LANES), bf16),
            pltpu.VMEM((PAIRS, 2, 4, piece, LANES), bf16),
            dma((13,)),
            dma((PAIRS, 2, 19)),
            dma((PAIRS, 2, 19)),
            dma((PAIRS, 8)),
            dma((PAIRS, 8)),
            dma((3,)),
            dma((3,)),
            dma((PAIRS, 2)),
        ],
        compiler_params=pltpu.CompilerParams(
            collective_id=0, has_side_effects=True, vmem_limit_bytes=60 << 20
        ),
    )(eigvec, force_const, amplitudes, mlip_forces, frequency)


def local(eigvec, force_const, amplitudes, mlip_forces, frequency):
    resid, disp = exchange(eigvec, force_const, amplitudes, mlip_forces, frequency)
    out_rows = force_const.shape[0]
    resid = resid.transpose(2, 3, 0, 1, 4).reshape(out_rows, -1)
    disp = disp.transpose(1, 0, 2).reshape(disp.shape[1], -1)
    total = lax.dot_general(resid, disp, (((1,), (1,)), ((), ())), preferred_element_type=jnp.float32)
    return total * (1.0 / 32.0)


def solution(mesh):
    return jax.shard_map(
        local,
        mesh=mesh,
        in_specs=(
            P("row", ("col", "cfg")),
            P(("col", "cfg"), "row"),
            P(("col", "cfg"), None),
            P(("col", "cfg"), "row"),
            P(("col", "cfg")),
        ),
        out_specs=P(("col", "cfg"), "row"),
        check_vma=False,
    )
```

time: 505 us -> 140 us (0.28)
  waiting for transfers between devices: 463 us -> 0 us
  Pallas kernels: 0 us -> 117 us
  matrix products: 23.6 us -> 6.92 us
  local copies, waits for them, and re-layouts: 0.93 us -> 14.6 us
  between operations: 13.1 us -> 0.02 us
    reduce_scatter x2 -> x0, waiting for transfers between devices: 281 us -> none  [the longest x1 217 us: local(): lax.psum_scatter(lax.dot_general(scaled_amp, eigvec, (((0,), (1,)), ((),...]
    all_gather x2 -> x0, waiting for transfers between devices: 182 us -> none  [the longest x1 148 us: local(): lax.all_gather(own_rows.astype(jnp.bfloat16), ('col', 'cfg'), axis=0, til...]
    pallas_call x0 -> x1, Pallas kernels: none -> 117 us  [exchange(): pl.pallas_call(comm_kernel, name='exchange', out_shape=[jax.ShapeDtypeStr...]
    dot_general x3 -> x1, matrix products: 23.6 us -> 6.92 us  [local(): lax.dot_general(resid, disp, (((1,), (1,)), ((), ())), preferred_element_...]
    transpose x0 -> x2, local copies, waits for them, and re-layouts: none -> 9.22 us  [the longest x1 6.73 us: local(): disp = disp.transpose(1, 0, 2).reshape(disp.shape[1], -1)]
  transfers between devices with their start and end apart: 4 -> 0, of which waited for: 4 -> 0; matrix products, arithmetic and copies ran while one was open for 0% -> 0% of each run, Pallas kernels for 0% -> 0%
where the time goes in v1:
time: 140 us; the launch traced here: 139 us
  Pallas kernels  117 us (84%)
  local copies, waits for them, and re-layouts  14.6 us (10%)
  matrix products  6.92 us (5%)
    pallas_call x1, Pallas kernels, exchange(): pl.pallas_call(comm_kernel, name='exchange', out_shape=[jax.ShapeDtypeStr...  117 us
    dot_general x1, matrix products, local(): lax.dot_general(resid, disp, (((1,), (1,)), ((), ())), preferred_element_...  6.92 us
    transpose x1, local copies, waits for them, and re-layouts, local(): disp = disp.transpose(1, 0, 2).reshape(disp.shape[1], -1)  6.73 us
    unnamed x1, local copies, waits for them, and re-layouts  4.5 us

profile of v1, /device:TPU:1, one launch (start us, length us, event | category | flops | bytes accessed | tf_op | source)
XLA Modules:
  0.0 138.9 jit_solution(12924984659451024939)
XLA Ops:
  0.0 4.5 %copy.7.eig_hbm = bf16[2304,576]{1,0:T(8,128)(2,1)} copy(bf16[2304,576]{0,1:T(8,128)(2,1)} %param.5) | data formatting | bytes 5308416 | tf_op args[0]
  4.5 117.4 %exchange.1 = (bf16[4,2,4,144,128]{4,3,2,1,0:T(8,128)(2,1)}, bf16[4,2304,256]{2,1,0:T(8,128)(2,1)}) custom-call(bf16[2304,576]{1,0:T(8,128)(2,1)} %copy.7.eig_hbm, bf16[576,2304]{1,0:T(8,128)(2,1)} %fc_hbm.1, bf16[576,1024]{1,0:T(8,128)(2,1)} %amp_hbm.1, bf16[576,128]{1,0:T(8,128)(2,1)} %forces_hbm.1, f32[576]{0:T(1024)} %freq_ref.1), custom_call_target="tpu_custom_call" | custom-call | tf_op jit(solution)/shard_map/exchange/pallas_call | solution.py:324
  121.9 2.5 %copy.8 = bf16[4,144,4,2,128]{4,3,2,1,0:T(2,128)(2,1)S(1)} copy(bf16[4,144,4,2,128]{4,1,0,3,2:T(8,128)(2,1)} %bitcast.7) | data formatting | bytes 2359296 | tf_op jit(solution)/shard_map/transpose | solution.py:375
  124.4 0.9 reshape.6
  125.2 6.7 %copy.9 = bf16[2304,4,256]{0,2,1:T(8,128)(2,1)} copy(bf16[2304,4,256]{2,0,1:T(8,128)(2,1)} %bitcast.5) | data formatting | bytes 9437184 | tf_op jit(solution)/shard_map/transpose | solution.py:376
  132.0 6.9 %convolution_multiply_fusion = f32[576,2304]{1,0:T(8,128)} fusion(bf16[576,1024]{1,0:T(8,128)(2,1)S(1)} %reshape.6, bf16[2304,1024]{0,1:T(8,128)(2,1)} %bitcast.6), kind=kOutput, calls=%fused_computation | convolution fusion | flops 2719236096 | bytes 11206656 | tf_op jit(solution)/shard_map/dot_general | solution.py:377

commit v2 on v1

v2 whole, which is shorter than its diff:
```python
import functools

import jax
import jax.numpy as jnp
from jax import lax
from jax.experimental import pallas as pl
from jax.experimental.pallas import tpu as pltpu
from jax.sharding import PartitionSpec as P

MESH = pl.DeviceIdType.MESH
PAIRS = 4
LANES = 128
TILE = 256
ORDER = [
    (0, 0), (1, 0, 0), (1, 0, 1), (0, 1), (2, 0, 0), (2, 0, 1), (1, 1, 0), (1, 1, 1),
    (0, 2), (0, 3), (3, 0, 0), (3, 0, 1), (2, 1, 0), (2, 1, 1), (1, 2, 0), (1, 2, 1),
    (4, 0, 0), (4, 0, 1), (1, 3, 0), (1, 3, 1), (3, 1, 0), (3, 1, 1), (2, 2, 0), (2, 2, 1),
    (5, 0, 0), (5, 0, 1), (4, 1, 0), (4, 1, 1), (2, 3, 0), (2, 3, 1), (3, 2, 0), (3, 2, 1),
    (6, 0, 1), (6, 0, 0), (4, 2, 0), (4, 2, 1), (5, 1, 0), (5, 1, 1), (3, 3, 0), (3, 3, 1),
    (7, 0), (5, 2, 0), (5, 2, 1), (4, 3, 0), (4, 3, 1), (8, 0), (6, 1, 1), (6, 1, 0),
    (6, 2, 1), (6, 2, 0), (5, 3, 0), (5, 3, 1), (9, 0), (7, 1), (7, 2), (8, 1),
    (6, 3, 1), (6, 3, 0), (8, 2), (7, 3), (10, 0), (8, 3), (11, 0), (12, 0, 0),
    (9, 1), (12, 0, 1), (12, 0, 2), (9, 2), (9, 3), (10, 1), (11, 1), (12, 1, 0),
    (12, 1, 1), (12, 1, 2), (10, 2), (11, 2), (12, 2, 0), (12, 2, 1), (10, 3), (12, 2, 2),
    (11, 3),
]


def comm_kernel(
    eig_hbm, fc_hbm, amp_hbm, forces_hbm, freq_ref, grad_hbm, resid_hbm, disp_hbm,
    eig_t, eig, fc, amp, scale, part32, part16, in_opp, in_near, sum32, sum16, in_second, own32, own16, in_zl,
    disp, harm, in_core, harm32, harm16, in_zh, force_in, force_own, resid, grad,
    load_sem, col_send, col_recv, row_send, row_recv, m_send, m_recv, out_sem,
):
    modes, rows = eig_hbm.shape
    quarter, sub = rows // 4, rows // 16
    half = quarter // 2
    out_rows = fc_hbm.shape[0]
    piece = out_rows // 4

    row, x, cfg = lax.axis_index("row"), lax.axis_index("col"), lax.axis_index("cfg")
    zh, core, y, zl = row // 2, row % 2, cfg // 2, cfg % 2

    def x_dev(d):
        return {"col": (x + d) % 4}

    def y_dev(d):
        return {"cfg": ((y + d) % 4) * 2 + zl}

    def zh_dev(d):
        return {"row": ((zh + d) % 4) * 2 + core}

    zl_dev = {"cfg": y * 2 + (1 - zl)}
    core_dev = {"row": zh * 2 + (1 - core)}
    axes = [(x, x_dev, y, y_dev), (y, y_dev, x, x_dev)]

    loads = [pltpu.make_async_copy(amp_hbm.at[:, pl.ds(p * 2 * LANES, 2 * LANES)], amp.at[p], load_sem.at[p]) for p in range(PAIRS)]
    loads += [pltpu.make_async_copy(eig_hbm.at[:, pl.ds(q * TILE, TILE)], eig_t.at[q], load_sem.at[13 + q]) for q in range(rows // TILE)]
    load_fc = pltpu.make_async_copy(fc_hbm, fc, load_sem.at[8])
    load_forces = [pltpu.make_async_copy(forces_hbm.at[pl.ds(q * piece, piece)], force_own.at[q], load_sem.at[9 + q]) for q in range(4)]
    for c in loads:
        c.start()
    for c in load_forces:
        c.start()
    load_fc.start()

    barrier = pltpu.get_barrier_semaphore()
    peers = [x_dev(1), x_dev(2), x_dev(3), y_dev(1), y_dev(2), y_dev(3), zh_dev(1), zh_dev(2), zh_dev(3), zl_dev, core_dev]
    for dev in peers:
        pl.semaphore_signal(barrier, inc=1, device_id=dev, device_id_type=MESH)

    f = freq_ref[...].reshape(1, modes)
    on_diag = lax.broadcasted_iota(jnp.int32, (modes, modes), 0) == lax.broadcasted_iota(jnp.int32, (modes, modes), 1)
    f_col = jnp.sum(jnp.where(on_diag, f, 0.0), axis=1, keepdims=True)
    scale[...] = jnp.broadcast_to(1.0 / jnp.sqrt(2.0 * f_col), scale.shape)

    for c in loads:
        c.wait()
    for c in load_forces:
        c.wait()

    def flip(q, carry):
        eig[pl.ds(pl.multiple_of(q * TILE, TILE), TILE)] = eig_t[q].T
        return carry

    lax.fori_loop(0, rows // TILE, flip, 0)

    def col_copy(p, t, k, src, dst, dev):
        return pltpu.make_async_remote_copy(
            src_ref=src, dst_ref=dst, send_sem=col_send.at[p, t, k], recv_sem=col_recv.at[p, t, k],
            device_id=dev, device_id_type=MESH,
        )

    def row_copy(p, k, src, dst, dev):
        return pltpu.make_async_remote_copy(
            src_ref=src, dst_ref=dst, send_sem=row_send.at[p, k], recv_sem=row_recv.at[p, k],
            device_id=dev, device_id_type=MESH,
        )

    lo, hi = pl.ds(0, half), pl.ds(half, half)

    def first_out(p, t, k):
        a, a_dev, _, _ = axes[t]
        q1, q2, q3 = (a + 1) % 4, (a + 2) % 4, (a + 3) % 4
        src, dst, dev = [
            (part16.at[p, t, q2, lo], in_opp.at[p, t, 0], 1),
            (part16.at[p, t, q2, hi], in_opp.at[p, t, 1], 3),
            (part16.at[p, t, q1, hi], in_near.at[p, t, 0, hi], 1),
            (part16.at[p, t, q3, lo], in_near.at[p, t, 1, lo], 3),
            (part16.at[p, t, q1, lo], in_near.at[p, t, 0, lo], 1),
            (part16.at[p, t, q3, hi], in_near.at[p, t, 1, hi], 3),
        ][k]
        return col_copy(p, t, k, src, dst, a_dev(dev))

    def second_out(p, t, d):
        _, _, b, b_dev = axes[t]
        return col_copy(p, t, 5 + d, sum16.at[p, t, (b + d) % 4], in_second.at[p, t, d - 1], b_dev(d))

    def zl_out(p, t):
        return col_copy(p, t, 9, own16.at[p, t], in_zl.at[p, t], zl_dev)

    def disp_at(p, t, start, size, align):
        return disp.at[p, t, pl.ds(pl.multiple_of(start, align), size)]

    def spread_b(p, t, d, owner):
        a, _, _, b_dev = axes[t]
        at = disp_at(p, t, a * quarter + owner * sub, sub, 16)
        return col_copy(p, t, 9 + d, at, at, b_dev(d))

    def spread_a(p, t, k, owner):
        _, a_dev, _, _ = axes[t]
        which, dev = [(0, 1), (1, 1), (1, 3), (0, 3), (0, 1), (1, 3)][k]
        at = disp_at(p, t, owner * quarter + which * half, half, 16)
        return col_copy(p, t, 13 + k, at, at, a_dev(dev))

    def core_out(p):
        return row_copy(p, 0, harm.at[p, 1 - core], in_core.at[p], core_dev)

    def zh_out(p, d):
        return row_copy(p, d, harm16.at[p, (zh + d) % 4], in_zh.at[p, d - 1], zh_dev(d))

    def resid_spread(p, d, owner):
        at = resid.at[p, core, pl.ds(pl.multiple_of(owner * piece, 16), piece)]
        return row_copy(p, 3 + d, at, at, zh_dev(d))

    def resid_core(p, which):
        at = resid.at[p, which]
        return row_copy(p, 7, at, at, core_dev)

    def disp_store(t):
        return pltpu.make_async_copy(disp.at[PAIRS - 1, t], disp_hbm.at[:, pl.ds(t * LANES, LANES)], out_sem.at[t])

    def resid_store(t):
        return pltpu.make_async_copy(resid.at[PAIRS - 1, t], resid_hbm.at[:, pl.ds(t * LANES, LANES)], out_sem.at[2 + t])

    def grad_store(g):
        at = pl.ds(g * 3 * TILE, 3 * TILE)
        return pltpu.make_async_copy(grad.at[:, at], grad_hbm.at[:, at], out_sem.at[4 + g])

    def force_out(d, slot):
        return pltpu.make_async_remote_copy(
            src_ref=force_own.at[(zh + d) % 4], dst_ref=force_in.at[slot],
            send_sem=m_send.at[d - 1], recv_sem=m_recv.at[d - 1], device_id=zh_dev(d), device_id_type=MESH,
        )

    def compute_part(p):
        scaled = (scale[:, :1] * amp[p].astype(jnp.float32)).astype(jnp.bfloat16)

        def one(q, carry):
            product = jnp.dot(eig[pl.ds(pl.multiple_of(q * quarter, 16), quarter)], scaled, preferred_element_type=jnp.float32)
            for t in range(2):
                block = product[:, t * LANES : (t + 1) * LANES]
                part32[p, t, q] = block
                part16[p, t, q] = block.astype(jnp.bfloat16)
            return carry

        lax.fori_loop(0, 4, one, 0)

    def send_part(p):
        for k in range(4):
            for t in range(2):
                first_out(p, t, k).start()

    def stage0(p):
        compute_part(p)
        if p == 0:
            pl.semaphore_wait(barrier, len(peers))
        send_part(p)
        if p == 0:
            for d in (1, 2, 3):
                force_out(d, zh).start()

    def stage1(p, t):
        a = axes[t][0]
        first_out(p, t, 0).wait_recv()
        q1, q3 = (a + 1) % 4, (a + 3) % 4
        part16[p, t, q1, lo] = (part32[p, t, q1, lo] + in_opp[p, t, 0].astype(jnp.float32)).astype(jnp.bfloat16)
        first_out(p, t, 4).start()
        first_out(p, t, 1).wait_recv()
        part16[p, t, q3, hi] = (part32[p, t, q3, hi] + in_opp[p, t, 1].astype(jnp.float32)).astype(jnp.bfloat16)
        first_out(p, t, 5).start()

    def stage2(p, t):
        a, _, b, _ = axes[t]
        for k in range(2, 6):
            first_out(p, t, k).wait_recv()
        total = part32[p, t, a] + in_near[p, t, 0].astype(jnp.float32) + in_near[p, t, 1].astype(jnp.float32)
        total = total.reshape(4, sub, LANES)
        sum32[p, t] = total
        sum16[p, t] = total.astype(jnp.bfloat16)
        for d in (2, 1, 3):
            second_out(p, t, d).start()

    def stage3(p, t):
        b = axes[t][2]
        for d in (1, 2, 3):
            second_out(p, t, d).wait_recv()
        total = sum32[p, t, b]
        for d in range(3):
            total += in_second[p, t, d].astype(jnp.float32)
        own32[p, t] = total
        own16[p, t] = total.astype(jnp.bfloat16)
        zl_out(p, t).start()

    def stage4(p, t):
        a, _, b, _ = axes[t]
        zl_out(p, t).wait_recv()
        value = (own32[p, t] + in_zl[p, t].astype(jnp.float32)).astype(jnp.bfloat16)
        disp[p, t, pl.ds(pl.multiple_of(a * quarter + b * sub, 16), sub)] = value
        for d in (2, 1, 3):
            spread_b(p, t, d, b).start()

    def stage5(p, t):
        a, _, b, _ = axes[t]
        for d in (1, 2, 3):
            spread_b(p, t, d, (b + 4 - d) % 4).wait_recv()
        for k in (0, 2, 1, 3):
            spread_a(p, t, k, a).start()

    def stage6(p, t):
        a = axes[t][0]
        below, above = (a + 3) % 4, (a + 1) % 4
        spread_a(p, t, 0, below).wait_recv()
        spread_a(p, t, 4, below).start()
        spread_a(p, t, 2, above).wait_recv()
        spread_a(p, t, 5, above).start()

    def stage7(p):
        for t in range(2):
            a = axes[t][0]
            below, above, far = (a + 3) % 4, (a + 1) % 4, (a + 2) % 4
            spread_a(p, t, 1, below).wait_recv()
            spread_a(p, t, 3, above).wait_recv()
            spread_a(p, t, 4, far).wait_recv()
            spread_a(p, t, 5, far).wait_recv()
        if p == PAIRS - 1:
            for t in range(2):
                disp_store(t).start()
        if p == 0:
            load_fc.wait()
            for d in (1, 2, 3):
                force_out(d, (zh + 4 - d) % 4).wait_recv()

        product = jnp.dot(fc[...], jnp.concatenate([disp[p, 0], disp[p, 1]], axis=1), preferred_element_type=jnp.float32)
        for t in range(2):
            harm[p, t] = product[:, t * LANES : (t + 1) * LANES]
        core_out(p).start()

    def stage8(p):
        core_out(p).wait_recv()
        total = (harm[p, core] + in_core[p]).reshape(4, piece, LANES)
        harm32[p] = total
        harm16[p] = total.astype(jnp.bfloat16)
        for d in (2, 1, 3):
            zh_out(p, d).start()

    def stage9(p):
        for d in (1, 2, 3):
            zh_out(p, d).wait_recv()
        total = force_in[p].astype(jnp.float32) + harm32[p, zh]
        for d in range(3):
            total += in_zh[p, d].astype(jnp.float32)
        resid[p, core, pl.ds(pl.multiple_of(zh * piece, 16), piece)] = total.astype(jnp.bfloat16)
        for d in (2, 1, 3):
            resid_spread(p, d, zh).start()

    def stage10(p):
        for d in (1, 2, 3):
            resid_spread(p, d, (zh + 4 - d) % 4).wait_recv()
        resid_core(p, core).start()

    def stage11(p):
        resid_core(p, 1 - core).wait_recv()
        if p == PAIRS - 1:
            for t in range(2):
                resid_store(t).start()

    def stage12(p, g):
        left = jnp.concatenate([resid[p, 0], resid[p, 1]], axis=1)
        for c in range(g * 3, g * 3 + 3):
            at = pl.ds(c * TILE, TILE)
            right = jnp.concatenate([disp[p, 0, at], disp[p, 1, at]], axis=1)
            term = lax.dot_general(left, right, (((1,), (1,)), ((), ())), preferred_element_type=jnp.float32)
            if p > 0:
                term += grad[:, at]
            grad[:, at] = term
        if p == PAIRS - 2:
            grad_store(g).start()

    stages = [stage0, stage1, stage2, stage3, stage4, stage5, stage6, stage7, stage8, stage9, stage10, stage11, stage12]
    force_in[zh] = force_own[zh]
    for s, *which in ORDER:
        stages[s](*which)

    def drain(p, carry):
        for t in range(2):
            a, _, b, _ = axes[t]
            for k in range(6):
                first_out(p, t, k).wait_send()
                spread_a(p, t, k, a).wait_send()
            for d in (1, 2, 3):
                second_out(p, t, d).wait_send()
                spread_b(p, t, d, b).wait_send()
            zl_out(p, t).wait_send()
        core_out(p).wait_send()
        for d in (1, 2, 3):
            zh_out(p, d).wait_send()
            resid_spread(p, d, zh).wait_send()
        resid_core(p, core).wait_send()
        return carry

    lax.fori_loop(0, PAIRS, drain, 0)
    for t in range(2):
        disp_store(t).wait()
        resid_store(t).wait()
    for g in range(3):
        grad_store(g).wait()
    for d in (1, 2, 3):
        force_out(d, zh).wait_send()


def exchange(eigvec, force_const, amplitudes, mlip_forces, frequency):
    modes, rows = eigvec.shape
    out_rows = force_const.shape[0]
    quarter, sub, piece = rows // 4, rows // 16, out_rows // 4
    half = quarter // 2
    bf16, f32 = jnp.bfloat16, jnp.float32
    anywhere = pl.BlockSpec(memory_space=pl.ANY)
    dma = pltpu.SemaphoreType.DMA
    return pl.pallas_call(
        comm_kernel,
        name="exchange",
        out_shape=[
            jax.ShapeDtypeStruct((out_rows, rows), f32),
            jax.ShapeDtypeStruct((out_rows, 2 * LANES), bf16),
            jax.ShapeDtypeStruct((rows, 2 * LANES), bf16),
        ],
        in_specs=[anywhere] * 4 + [pl.BlockSpec(memory_space=pltpu.VMEM)],
        out_specs=[anywhere] * 3,
        scratch_shapes=[
            pltpu.VMEM((rows // TILE, modes, TILE), bf16),
            pltpu.VMEM((rows, modes), bf16),
            pltpu.VMEM((out_rows, rows), bf16),
            pltpu.VMEM((PAIRS, modes, 2 * LANES), bf16),
            pltpu.VMEM((modes, LANES), f32),
            pltpu.VMEM((PAIRS, 2, 4, quarter, LANES), f32),
            pltpu.VMEM((PAIRS, 2, 4, quarter, LANES), bf16),
            pltpu.VMEM((PAIRS, 2, 2, half, LANES), bf16),
            pltpu.VMEM((PAIRS, 2, 2, quarter, LANES), bf16),
            pltpu.VMEM((PAIRS, 2, 4, sub, LANES), f32),
            pltpu.VMEM((PAIRS, 2, 4, sub, LANES), bf16),
            pltpu.VMEM((PAIRS, 2, 3, sub, LANES), bf16),
            pltpu.VMEM((PAIRS, 2, sub, LANES), f32),
            pltpu.VMEM((PAIRS, 2, sub, LANES), bf16),
            pltpu.VMEM((PAIRS, 2, sub, LANES), bf16),
            pltpu.VMEM((PAIRS, 2, rows, LANES), bf16),
            pltpu.VMEM((PAIRS, 2, out_rows, LANES), f32),
            pltpu.VMEM((PAIRS, out_rows, LANES), f32),
            pltpu.VMEM((PAIRS, 4, piece, LANES), f32),
            pltpu.VMEM((PAIRS, 4, piece, LANES), bf16),
            pltpu.VMEM((PAIRS, 3, piece, LANES), bf16),
            pltpu.VMEM((PAIRS, piece, LANES), bf16),
            pltpu.VMEM((4, piece, LANES), bf16),
            pltpu.VMEM((PAIRS, 2, out_rows, LANES), bf16),
            pltpu.VMEM((out_rows, rows), f32),
            dma((13 + rows // TILE,)),
            dma((PAIRS, 2, 19)),
            dma((PAIRS, 2, 19)),
            dma((PAIRS, 8)),
            dma((PAIRS, 8)),
            dma((3,)),
            dma((3,)),
            dma((7,)),
        ],
        compiler_params=pltpu.CompilerParams(
            collective_id=0, has_side_effects=True, vmem_limit_bytes=60 << 20
        ),
    )(eigvec, force_const, amplitudes, mlip_forces, frequency)


def last_kernel(grad, resid, disp, out):
    term = lax.dot_general(resid[...], disp[...], (((1,), (1,)), ((), ())), preferred_element_type=jnp.float32)
    out[...] = (grad[...] + term) * (1.0 / 32.0)


def add_last(grad, resid, disp):
    out_rows, rows = grad.shape
    configs = resid.shape[1]
    tile = out_rows // 6
    return pl.pallas_call(
        last_kernel,
        name="add_last",
        grid=(6,),
        out_shape=jax.ShapeDtypeStruct((out_rows, rows), jnp.float32),
        in_specs=[
            pl.BlockSpec((tile, rows), lambda i: (i, 0)),
            pl.BlockSpec((tile, configs), lambda i: (i, 0)),
            pl.BlockSpec((rows, configs), lambda i: (0, 0)),
        ],
        out_specs=pl.BlockSpec((tile, rows), lambda i: (i, 0)),
        compiler_params=pltpu.CompilerParams(vmem_limit_bytes=60 << 20),
    )(grad, resid, disp)


def local(eigvec, force_const, amplitudes, mlip_forces, frequency):
    return add_last(*exchange(eigvec.T, force_const, amplitudes, mlip_forces, frequency))


def solution(mesh):
    return jax.shard_map(
        local,
        mesh=mesh,
        in_specs=(
            P("row", ("col", "cfg")),
            P(("col", "cfg"), "row"),
            P(("col", "cfg"), None),
            P(("col", "cfg"), "row"),
            P(("col", "cfg")),
        ),
        out_specs=P(("col", "cfg"), "row"),
        check_vma=False,
    )
```

time: 140 us -> 101 us (0.72)
  Pallas kernels: 117 us -> 101 us
  local copies, waits for them, and re-layouts: 14.6 us -> 0 us
  matrix products: 6.92 us -> 0 us
    pallas_call x1, Pallas kernels: 117 us -> 92.5 us  [exchange(): pl.pallas_call(comm_kernel, name='exchange', out_shape=[jax.ShapeDtypeStr...]
    transpose x2 -> x0, local copies, waits for them, and re-layouts: 9.22 us -> none  [the longest x1 6.73 us: local(): disp = disp.transpose(1, 0, 2).reshape(disp.shape[1], -1)]
    pallas_call x0 -> x1, Pallas kernels: none -> 8.11 us  [add_last(): pl.pallas_call(last_kernel, name='add_last', grid=(6,), out_shape=jax.Sha...]
    dot_general x1 -> x0, matrix products: 6.92 us -> none  [local(): lax.dot_general(resid, disp, (((1,), (1,)), ((), ())), preferred_element_...]
    unnamed x1 -> x0, local copies, waits for them, and re-layouts: 4.5 us -> none
where the time goes in v2:
time: 101 us
  Pallas kernels  101 us (100%)
    pallas_call x1, Pallas kernels, exchange(): pl.pallas_call(comm_kernel, name='exchange', out_shape=[jax.ShapeDtypeStr...  92.5 us
    pallas_call x1, Pallas kernels, add_last(): pl.pallas_call(last_kernel, name='add_last', grid=(6,), out_shape=jax.Sha...  8.11 us

profile of v2, /device:TPU:1, one launch (start us, length us, event | category | flops | bytes accessed | tf_op | source)
XLA Modules:
  0.0 100.6 jit_solution(17423697040140864379)
XLA Ops:
  0.0 92.5 %exchange.1 = (f32[576,2304]{1,0:T(8,128)}, bf16[576,256]{1,0:T(8,128)(2,1)}, bf16[2304,256]{1,0:T(8,128)(2,1)}) custom-call(bf16[576,2304]{1,0:T(8,128)(2,1)} %bitcast.1, bf16[576,2304]{1,0:T(8,128)(2,1)} %fc_hbm.1, bf16[576,1024]{1,0:T(8,128)(2,1)} %amp_hbm.1, bf16[576,128]{1,0:T(8,128)(2,1)} %forces_hbm.1, f32[576]{0:T(1024)} %freq_ref.1), custom_call_target="tpu_custom_call" | custom-call | tf_op jit(solution)/shard_map/exchange/pallas_call | solution.py:350
  92.5 8.1 %add_last.1 = f32[576,2304]{1,0:T(8,128)} custom-call(f32[576,2304]{1,0:T(8,128)} %get-tuple-element.8.grad, bf16[576,256]{1,0:T(8,128)(2,1)} %get-tuple-element.9.resid, bf16[2304,256]{1,0:T(8,128)(2,1)} %get-tuple-element.10.disp), custom_call_target="tpu_custom_call" | custom-call | tf_op jit(solution)/shard_map/add_last/pallas_call | solution.py:410

commit v3 on v2

--- a/solution.py
+++ b/solution.py
@@ -12,17 +12,17 @@
 LANES = 128
 TILE = 256
 ORDER = [
-    (0, 0), (1, 0, 0), (1, 0, 1), (0, 1), (2, 0, 0), (2, 0, 1), (1, 1, 0), (1, 1, 1),
-    (0, 2), (0, 3), (3, 0, 0), (3, 0, 1), (2, 1, 0), (2, 1, 1), (1, 2, 0), (1, 2, 1),
-    (4, 0, 0), (4, 0, 1), (1, 3, 0), (1, 3, 1), (3, 1, 0), (3, 1, 1), (2, 2, 0), (2, 2, 1),
-    (5, 0, 0), (5, 0, 1), (4, 1, 0), (4, 1, 1), (2, 3, 0), (2, 3, 1), (3, 2, 0), (3, 2, 1),
-    (6, 0, 1), (6, 0, 0), (4, 2, 0), (4, 2, 1), (5, 1, 0), (5, 1, 1), (3, 3, 0), (3, 3, 1),
-    (7, 0), (5, 2, 0), (5, 2, 1), (4, 3, 0), (4, 3, 1), (8, 0), (6, 1, 1), (6, 1, 0),
-    (6, 2, 1), (6, 2, 0), (5, 3, 0), (5, 3, 1), (9, 0), (7, 1), (7, 2), (8, 1),
-    (6, 3, 1), (6, 3, 0), (8, 2), (7, 3), (10, 0), (8, 3), (11, 0), (12, 0, 0),
-    (9, 1), (12, 0, 1), (12, 0, 2), (9, 2), (9, 3), (10, 1), (11, 1), (12, 1, 0),
-    (12, 1, 1), (12, 1, 2), (10, 2), (11, 2), (12, 2, 0), (12, 2, 1), (10, 3), (12, 2, 2),
-    (11, 3),
+    (0, 0), (0, 2), (1, 2, 0), (1, 2, 1), (0, 1), (1, 0, 1), (2, 2, 1), (1, 0, 0),
+    (2, 2, 0), (1, 1, 1), (0, 3), (3, 2, 1), (2, 0, 1), (3, 2, 0), (2, 0, 0), (1, 1, 0),
+    (1, 3, 1), (4, 2, 1), (4, 2, 0), (3, 0, 1), (2, 1, 1), (2, 1, 0), (1, 3, 0), (3, 0, 0),
+    (5, 2, 1), (4, 0, 1), (5, 2, 0), (2, 3, 1), (3, 1, 1), (4, 0, 0), (2, 3, 0), (3, 1, 0),
+    (6, 2, 1), (6, 2, 0), (5, 0, 1), (5, 0, 0), (4, 1, 0), (4, 1, 1), (3, 3, 1), (3, 3, 0),
+    (7, 2), (6, 0, 1), (6, 0, 0), (4, 3, 0), (4, 3, 1), (8, 2), (5, 1, 0), (5, 1, 1),
+    (7, 0), (6, 1, 1), (6, 1, 0), (8, 0), (5, 3, 1), (5, 3, 0), (9, 2, 1), (9, 2, 0),
+    (7, 1), (6, 3, 1), (6, 3, 0), (9, 0, 0), (9, 0, 1), (8, 1), (7, 3), (10, 2),
+    (8, 3), (11, 2), (10, 0), (9, 1, 0), (9, 1, 1), (11, 0), (12, 2, 0), (9, 3, 0),
+    (9, 3, 1), (12, 0, 0), (12, 0, 1), (12, 2, 1), (10, 1), (12, 0, 2), (12, 2, 2), (11, 1),
+    (12, 1, 0), (10, 3), (12, 1, 1), (12, 1, 2), (11, 3),
 ]
 
 
@@ -54,15 +54,12 @@
     core_dev = {"row": zh * 2 + (1 - core)}
     axes = [(x, x_dev, y, y_dev), (y, y_dev, x, x_dev)]
 
-    loads = [pltpu.make_async_copy(amp_hbm.at[:, pl.ds(p * 2 * LANES, 2 * LANES)], amp.at[p], load_sem.at[p]) for p in range(PAIRS)]
-    loads += [pltpu.make_async_copy(eig_hbm.at[:, pl.ds(q * TILE, TILE)], eig_t.at[q], load_sem.at[13 + q]) for q in range(rows // TILE)]
+    load_amp = [pltpu.make_async_copy(amp_hbm.at[:, pl.ds(p * 2 * LANES, 2 * LANES)], amp.at[p], load_sem.at[p]) for p in range(PAIRS)]
+    load_eig = [pltpu.make_async_copy(eig_hbm.at[:, pl.ds(q * TILE, TILE)], eig_t.at[q], load_sem.at[13 + q]) for q in range(rows // TILE)]
     load_fc = pltpu.make_async_copy(fc_hbm, fc, load_sem.at[8])
     load_forces = [pltpu.make_async_copy(forces_hbm.at[pl.ds(q * piece, piece)], force_own.at[q], load_sem.at[9 + q]) for q in range(4)]
-    for c in loads:
+    for c in load_amp[:1] + load_eig + load_amp[1:] + load_forces + [load_fc]:
         c.start()
-    for c in load_forces:
-        c.start()
-    load_fc.start()
 
     barrier = pltpu.get_barrier_semaphore()
     peers = [x_dev(1), x_dev(2), x_dev(3), y_dev(1), y_dev(2), y_dev(3), zh_dev(1), zh_dev(2), zh_dev(3), zl_dev, core_dev]
@@ -74,16 +71,10 @@
     f_col = jnp.sum(jnp.where(on_diag, f, 0.0), axis=1, keepdims=True)
     scale[...] = jnp.broadcast_to(1.0 / jnp.sqrt(2.0 * f_col), scale.shape)
 
-    for c in loads:
+    for q, c in enumerate(load_eig):
         c.wait()
-    for c in load_forces:
-        c.wait()
-
-    def flip(q, carry):
-        eig[pl.ds(pl.multiple_of(q * TILE, TILE), TILE)] = eig_t[q].T
-        return carry
-
-    lax.fori_loop(0, rows // TILE, flip, 0)
+        eig[pl.ds(q * TILE, TILE)] = eig_t[q].T
+    load_amp[0].wait()
 
     def col_copy(p, t, k, src, dst, dev):
         return pltpu.make_async_remote_copy(
@@ -136,16 +127,24 @@
     def core_out(p):
         return row_copy(p, 0, harm.at[p, 1 - core], in_core.at[p], core_dev)
 
-    def zh_out(p, d):
-        return row_copy(p, d, harm16.at[p, (zh + d) % 4], in_zh.at[p, d - 1], zh_dev(d))
-
-    def resid_spread(p, d, owner):
-        at = resid.at[p, core, pl.ds(pl.multiple_of(owner * piece, 16), piece)]
-        return row_copy(p, 3 + d, at, at, zh_dev(d))
+    cut = piece // 32 * 16
+    portions = [(0, piece - cut), (piece - cut, cut)]
+
+    def zh_out(p, d, h):
+        at = pl.ds(*portions[h])
+        return row_copy(p, 2 * d - 1 + h, harm16.at[p, (zh + d) % 4, at], in_zh.at[p, d - 1, at], zh_dev(d))
+
+    def resid_rows(owner, h):
+        start, size = portions[h]
+        return pl.ds(pl.multiple_of(owner * piece + start, 16), size)
+
+    def resid_spread(p, d, h, owner):
+        at = resid.at[p, core, resid_rows(owner, h)]
+        return row_copy(p, 2 * d + 5 + h, at, at, zh_dev(d))
 
     def resid_core(p, which):
         at = resid.at[p, which]
-        return row_copy(p, 7, at, at, core_dev)
+        return row_copy(p, 13, at, at, core_dev)
 
     def disp_store(t):
         return pltpu.make_async_copy(disp.at[PAIRS - 1, t], disp_hbm.at[:, pl.ds(t * LANES, LANES)], out_sem.at[t])
@@ -163,7 +162,34 @@
             send_sem=m_send.at[d - 1], recv_sem=m_recv.at[d - 1], device_id=zh_dev(d), device_id_type=MESH,
         )
 
+    def first_part():
+        scaled = (scale[:, :1] * amp[0].astype(jnp.float32)).astype(jnp.bfloat16)
+
+        def one(t, d):
+            q = (axes[t][0] + d) % 4
+            block = jnp.dot(
+                eig[pl.ds(pl.multiple_of(q * quarter, 16), quarter)],
+                scaled[:, t * LANES : (t + 1) * LANES],
+                preferred_element_type=jnp.float32,
+            )
+            part32[0, t, q] = block
+            part16[0, t, q] = block.astype(jnp.bfloat16)
+
+        for t in range(2):
+            one(t, 2)
+        pl.semaphore_wait(barrier, len(peers))
+        for k in range(2):
+            for t in range(2):
+                first_out(0, t, k).start()
+        for d, k in ((1, 2), (3, 3)):
+            for t in range(2):
+                one(t, d)
+                first_out(0, t, k).start()
+        for t in range(2):
+            one(t, 0)
+
     def compute_part(p):
+        load_amp[p].wait()
         scaled = (scale[:, :1] * amp[p].astype(jnp.float32)).astype(jnp.bfloat16)
 
         def one(q, carry):
@@ -181,14 +207,20 @@
             for t in range(2):
                 first_out(p, t, k).start()
 
+    harm_first = [step[1] for step in ORDER if step[0] == 7][0]
+    grad_pairs = [[step[1] for step in ORDER if step[0] == 12 and step[2] == g] for g in range(3)]
+
     def stage0(p):
-        compute_part(p)
         if p == 0:
-            pl.semaphore_wait(barrier, len(peers))
-        send_part(p)
-        if p == 0:
+            first_part()
+            for c in load_forces:
+                c.wait()
+            force_in[zh] = force_own[zh]
             for d in (1, 2, 3):
                 force_out(d, zh).start()
+        else:
+            compute_part(p)
+            send_part(p)
 
     def stage1(p, t):
         a = axes[t][0]
@@ -256,7 +288,7 @@
         if p == PAIRS - 1:
             for t in range(2):
                 disp_store(t).start()
-        if p == 0:
+        if p == harm_first:
             load_fc.wait()
             for d in (1, 2, 3):
                 force_out(d, (zh + 4 - d) % 4).wait_recv()
@@ -271,22 +303,25 @@
         total = (harm[p, core] + in_core[p]).reshape(4, piece, LANES)
         harm32[p] = total
         harm16[p] = total.astype(jnp.bfloat16)
+        for h in range(2):
+            for d in (2, 1, 3):
+                zh_out(p, d, h).start()
+
+    def stage9(p, h):
+        for d in (1, 2, 3):
+            zh_out(p, d, h).wait_recv()
+        at = pl.ds(*portions[h])
+        total = force_in[p, at].astype(jnp.float32) + harm32[p, zh, at]
+        for d in range(3):
+            total += in_zh[p, d, at].astype(jnp.float32)
+        resid[p, core, resid_rows(zh, h)] = total.astype(jnp.bfloat16)
         for d in (2, 1, 3):
-            zh_out(p, d).start()
-
-    def stage9(p):
-        for d in (1, 2, 3):
-            zh_out(p, d).wait_recv()
-        total = force_in[p].astype(jnp.float32) + harm32[p, zh]
-        for d in range(3):
-            total += in_zh[p, d].astype(jnp.float32)
-        resid[p, core, pl.ds(pl.multiple_of(zh * piece, 16), piece)] = total.astype(jnp.bfloat16)
-        for d in (2, 1, 3):
-            resid_spread(p, d, zh).start()
+            resid_spread(p, d, h, zh).start()
 
     def stage10(p):
-        for d in (1, 2, 3):
-            resid_spread(p, d, (zh + 4 - d) % 4).wait_recv()
+        for h in range(2):
+            for d in (1, 2, 3):
+                resid_spread(p, d, h, (zh + 4 - d) % 4).wait_recv()
         resid_core(p, core).start()
 
     def stage11(p):
@@ -301,14 +336,13 @@
             at = pl.ds(c * TILE, TILE)
             right = jnp.concatenate([disp[p, 0, at], disp[p, 1, at]], axis=1)
             term = lax.dot_general(left, right, (((1,), (1,)), ((), ())), preferred_element_type=jnp.float32)
-            if p > 0:
+            if p != grad_pairs[g][0]:
                 term += grad[:, at]
             grad[:, at] = term
-        if p == PAIRS - 2:
+        if p == grad_pairs[g][-1]:
             grad_store(g).start()
 
     stages = [stage0, stage1, stage2, stage3, stage4, stage5, stage6, stage7, stage8, stage9, stage10, stage11, stage12]
-    force_in[zh] = force_own[zh]
     for s, *which in ORDER:
         stages[s](*which)
 
@@ -323,9 +357,10 @@
                 spread_b(p, t, d, b).wait_send()
             zl_out(p, t).wait_send()
         core_out(p).wait_send()
-        for d in (1, 2, 3):
-            zh_out(p, d).wait_send()
-            resid_spread(p, d, zh).wait_send()
+        for h in range(2):
+            for d in (1, 2, 3):
+                zh_out(p, d, h).wait_send()
+                resid_spread(p, d, h, zh).wait_send()
         resid_core(p, core).wait_send()
         return carry
 
@@ -386,8 +421,8 @@
             dma((13 + rows // TILE,)),
             dma((PAIRS, 2, 19)),
             dma((PAIRS, 2, 19)),
-            dma((PAIRS, 8)),
-            dma((PAIRS, 8)),
+            dma((PAIRS, 14)),
+            dma((PAIRS, 14)),
             dma((3,)),
             dma((3,)),
             dma((7,)),
@@ -398,26 +433,52 @@
     )(eigvec, force_const, amplitudes, mlip_forces, frequency)
 
 
-def last_kernel(grad, resid, disp, out):
-    term = lax.dot_general(resid[...], disp[...], (((1,), (1,)), ((), ())), preferred_element_type=jnp.float32)
-    out[...] = (grad[...] + term) * (1.0 / 32.0)
+def last_kernel(grad_hbm, resid_hbm, disp_hbm, out_hbm, grad, resid, disp, total, load_sem, store_sem):
+    tiles = disp.shape[0] // TILE
+
+    def load_grad(c):
+        at = pl.ds(c * TILE, TILE)
+        return pltpu.make_async_copy(grad_hbm.at[:, at], grad.at[:, at], load_sem.at[c])
+
+    def store(c):
+        at = pl.ds(c * TILE, TILE)
+        return pltpu.make_async_copy(total.at[:, at], out_hbm.at[:, at], store_sem.at[c])
+
+    load_resid = pltpu.make_async_copy(resid_hbm, resid, load_sem.at[tiles])
+    load_disp = pltpu.make_async_copy(disp_hbm, disp, load_sem.at[tiles + 1])
+    load_resid.start()
+    load_disp.start()
+    for c in range(tiles):
+        load_grad(c).start()
+    load_resid.wait()
+    load_disp.wait()
+    for c in range(tiles):
+        at = pl.ds(c * TILE, TILE)
+        term = lax.dot_general(resid[...], disp[at], (((1,), (1,)), ((), ())), preferred_element_type=jnp.float32)
+        load_grad(c).wait()
+        total[:, at] = (grad[:, at] + term) * (1.0 / 32.0)
+        store(c).start()
+    for c in range(tiles):
+        store(c).wait()
 
 
 def add_last(grad, resid, disp):
-    out_rows, rows = grad.shape
-    configs = resid.shape[1]
-    tile = out_rows // 6
+    anywhere = pl.BlockSpec(memory_space=pl.ANY)
+    tiles = disp.shape[0] // TILE
     return pl.pallas_call(
         last_kernel,
         name="add_last",
-        grid=(6,),
-        out_shape=jax.ShapeDtypeStruct((out_rows, rows), jnp.float32),
-        in_specs=[
-            pl.BlockSpec((tile, rows), lambda i: (i, 0)),
-            pl.BlockSpec((tile, configs), lambda i: (i, 0)),
-            pl.BlockSpec((rows, configs), lambda i: (0, 0)),
+        out_shape=jax.ShapeDtypeStruct(grad.shape, jnp.float32),
+        in_specs=[anywhere] * 3,
+        out_specs=anywhere,
+        scratch_shapes=[
+            pltpu.VMEM(grad.shape, jnp.float32),
+            pltpu.VMEM(resid.shape, jnp.bfloat16),
+            pltpu.VMEM(disp.shape, jnp.bfloat16),
+            pltpu.VMEM(grad.shape, jnp.float32),
+            pltpu.SemaphoreType.DMA((tiles + 2,)),
+            pltpu.SemaphoreType.DMA((tiles,)),
         ],
-        out_specs=pl.BlockSpec((tile, rows), lambda i: (i, 0)),
         compiler_params=pltpu.CompilerParams(vmem_limit_bytes=60 << 20),
     )(grad, resid, disp)
 

time: 101 us -> 98.4 us (0.974)
  Pallas kernels: 101 us -> 98.1 us
    pallas_call x1, Pallas kernels: 8.11 us -> 5.6 us  [add_last(): pl.pallas_call(last_kernel, name='add_last', out_shape=jax.ShapeDtypeStru...]
where the time goes in v3:
time: 98.4 us; the launch traced here: 98.3 us
  Pallas kernels  98.1 us (100%)
    pallas_call x1, Pallas kernels, exchange(): pl.pallas_call(comm_kernel, name='exchange', out_shape=[jax.ShapeDtypeStr...  92.5 us
    pallas_call x1, Pallas kernels, add_last(): pl.pallas_call(last_kernel, name='add_last', out_shape=jax.ShapeDtypeStru...  5.6 us

profile of v3, /device:TPU:1, one launch (start us, length us, event | category | flops | bytes accessed | tf_op | source)
XLA Modules:
  0.0 98.3 jit_solution(5643889277769201203)
XLA Ops:
  0.0 92.5 %exchange.1 = (f32[576,2304]{1,0:T(8,128)}, bf16[576,256]{1,0:T(8,128)(2,1)}, bf16[2304,256]{1,0:T(8,128)(2,1)}) custom-call(bf16[576,2304]{1,0:T(8,128)(2,1)} %bitcast.1, bf16[576,2304]{1,0:T(8,128)(2,1)} %fc_hbm.1, bf16[576,1024]{1,0:T(8,128)(2,1)} %amp_hbm.1, bf16[576,128]{1,0:T(8,128)(2,1)} %forces_hbm.1, f32[576]{0:T(1024)} %freq_ref.1), custom_call_target="tpu_custom_call" | custom-call | tf_op jit(solution)/shard_map/exchange/pallas_call | solution.py:385
  92.5 5.6 %add_last.1 = f32[576,2304]{1,0:T(8,128)} custom-call(f32[576,2304]{1,0:T(8,128)} %get-tuple-element.8.grad_hbm, bf16[576,256]{1,0:T(8,128)(2,1)} %get-tuple-element.9.resid_hbm, bf16[2304,256]{1,0:T(8,128)(2,1)} %get-tuple-element.10.disp_hbm), custom_call_target="tpu_custom_call" | custom-call | tf_op jit(solution)/shard_map/add_last/pallas_call | solution.py:468

commit v4 on v3

--- a/solution.py
+++ b/solution.py
@@ -12,17 +12,17 @@
 LANES = 128
 TILE = 256
 ORDER = [
-    (0, 0), (0, 2), (1, 2, 0), (1, 2, 1), (0, 1), (1, 0, 1), (2, 2, 1), (1, 0, 0),
-    (2, 2, 0), (1, 1, 1), (0, 3), (3, 2, 1), (2, 0, 1), (3, 2, 0), (2, 0, 0), (1, 1, 0),
-    (1, 3, 1), (4, 2, 1), (4, 2, 0), (3, 0, 1), (2, 1, 1), (2, 1, 0), (1, 3, 0), (3, 0, 0),
-    (5, 2, 1), (4, 0, 1), (5, 2, 0), (2, 3, 1), (3, 1, 1), (4, 0, 0), (2, 3, 0), (3, 1, 0),
-    (6, 2, 1), (6, 2, 0), (5, 0, 1), (5, 0, 0), (4, 1, 0), (4, 1, 1), (3, 3, 1), (3, 3, 0),
-    (7, 2), (6, 0, 1), (6, 0, 0), (4, 3, 0), (4, 3, 1), (8, 2), (5, 1, 0), (5, 1, 1),
-    (7, 0), (6, 1, 1), (6, 1, 0), (8, 0), (5, 3, 1), (5, 3, 0), (9, 2, 1), (9, 2, 0),
-    (7, 1), (6, 3, 1), (6, 3, 0), (9, 0, 0), (9, 0, 1), (8, 1), (7, 3), (10, 2),
-    (8, 3), (11, 2), (10, 0), (9, 1, 0), (9, 1, 1), (11, 0), (12, 2, 0), (9, 3, 0),
-    (9, 3, 1), (12, 0, 0), (12, 0, 1), (12, 2, 1), (10, 1), (12, 0, 2), (12, 2, 2), (11, 1),
-    (12, 1, 0), (10, 3), (12, 1, 1), (12, 1, 2), (11, 3),
+    (0, 0), (0, 1), (1, 0, 1), (1, 0, 0), (0, 3), (1, 1, 0), (1, 1, 1), (2, 0, 0),
+    (2, 0, 1), (0, 2), (2, 1, 0), (2, 1, 1), (3, 0, 1), (3, 0, 0), (1, 2, 0), (1, 2, 1),
+    (1, 3, 1), (4, 0, 1), (1, 3, 0), (4, 0, 0), (3, 1, 1), (3, 1, 0), (2, 2, 0), (2, 2, 1),
+    (5, 0, 1), (4, 1, 1), (5, 0, 0), (4, 1, 0), (2, 3, 1), (3, 2, 1), (2, 3, 0), (6, 0, 1),
+    (3, 2, 0), (5, 1, 1), (6, 0, 0), (5, 1, 0), (4, 2, 1), (3, 3, 0), (3, 3, 1), (4, 2, 0),
+    (7, 0), (6, 1, 0), (6, 1, 1), (4, 3, 1), (4, 3, 0), (5, 2, 0), (5, 2, 1), (8, 0),
+    (7, 1), (6, 2, 0), (6, 2, 1), (5, 3, 0), (8, 1), (5, 3, 1), (9, 0, 0), (7, 2),
+    (6, 3, 0), (6, 3, 1), (9, 0, 1), (9, 1, 0), (9, 1, 1), (8, 2), (7, 3), (10, 0),
+    (8, 3), (11, 0), (10, 1), (12, 0, 0), (9, 2, 0), (12, 0, 1), (9, 2, 1), (11, 1),
+    (12, 1, 0), (9, 3, 0), (9, 3, 1), (12, 0, 2), (12, 1, 1), (10, 2), (12, 1, 2), (11, 2),
+    (12, 2, 0), (10, 3), (12, 2, 1), (12, 2, 2), (11, 3),
 ]
 
 
@@ -58,7 +58,7 @@
     load_eig = [pltpu.make_async_copy(eig_hbm.at[:, pl.ds(q * TILE, TILE)], eig_t.at[q], load_sem.at[13 + q]) for q in range(rows // TILE)]
     load_fc = pltpu.make_async_copy(fc_hbm, fc, load_sem.at[8])
     load_forces = [pltpu.make_async_copy(forces_hbm.at[pl.ds(q * piece, piece)], force_own.at[q], load_sem.at[9 + q]) for q in range(4)]
-    for c in load_amp[:1] + load_eig + load_amp[1:] + load_forces + [load_fc]:
+    for c in load_amp[:1] + load_eig:
         c.start()
 
     barrier = pltpu.get_barrier_semaphore()
@@ -74,6 +74,8 @@
     for q, c in enumerate(load_eig):
         c.wait()
         eig[pl.ds(q * TILE, TILE)] = eig_t[q].T
+    for c in load_amp[1:] + load_forces + [load_fc]:
+        c.start()
     load_amp[0].wait()
 
     def col_copy(p, t, k, src, dst, dev):
@@ -445,15 +447,19 @@
         return pltpu.make_async_copy(total.at[:, at], out_hbm.at[:, at], store_sem.at[c])
 
     load_resid = pltpu.make_async_copy(resid_hbm, resid, load_sem.at[tiles])
-    load_disp = pltpu.make_async_copy(disp_hbm, disp, load_sem.at[tiles + 1])
+
+    def load_disp(c):
+        at = pl.ds(c * TILE, TILE)
+        return pltpu.make_async_copy(disp_hbm.at[at], disp.at[at], load_sem.at[tiles + 1 + c])
+
     load_resid.start()
-    load_disp.start()
     for c in range(tiles):
+        load_disp(c).start()
         load_grad(c).start()
     load_resid.wait()
-    load_disp.wait()
     for c in range(tiles):
         at = pl.ds(c * TILE, TILE)
+        load_disp(c).wait()
         term = lax.dot_general(resid[...], disp[at], (((1,), (1,)), ((), ())), preferred_element_type=jnp.float32)
         load_grad(c).wait()
         total[:, at] = (grad[:, at] + term) * (1.0 / 32.0)
@@ -476,7 +482,7 @@
             pltpu.VMEM(resid.shape, jnp.bfloat16),
             pltpu.VMEM(disp.shape, jnp.bfloat16),
             pltpu.VMEM(grad.shape, jnp.float32),
-            pltpu.SemaphoreType.DMA((tiles + 2,)),
+            pltpu.SemaphoreType.DMA((2 * tiles + 1,)),
             pltpu.SemaphoreType.DMA((tiles,)),
         ],
         compiler_params=pltpu.CompilerParams(vmem_limit_bytes=60 << 20),

time: 98.4 us -> 96.5 us (0.981)
  Pallas kernels: 98.1 us -> 96.2 us
    pallas_call x1, Pallas kernels: 92.5 us -> 90.7 us  [exchange(): pl.pallas_call(comm_kernel, name='exchange', out_shape=[jax.ShapeDtypeStr...]
where the time goes in v4:
time: 96.5 us; the launch traced here: 96.3 us
  Pallas kernels  96.2 us (100%)
    pallas_call x1, Pallas kernels, exchange(): pl.pallas_call(comm_kernel, name='exchange', out_shape=[jax.ShapeDtypeStr...  90.7 us
    pallas_call x1, Pallas kernels, add_last(): pl.pallas_call(last_kernel, name='add_last', out_shape=jax.ShapeDtypeStru...  5.51 us

profile of v4, /device:TPU:1, one launch (start us, length us, event | category | flops | bytes accessed | tf_op | source)
XLA Modules:
  0.0 96.3 jit_solution(14385336298424179722)
XLA Ops:
  0.0 90.7 %exchange.1 = (f32[576,2304]{1,0:T(8,128)}, bf16[576,256]{1,0:T(8,128)(2,1)}, bf16[2304,256]{1,0:T(8,128)(2,1)}) custom-call(bf16[576,2304]{1,0:T(8,128)(2,1)} %bitcast.1, bf16[576,2304]{1,0:T(8,128)(2,1)} %fc_hbm.1, bf16[576,1024]{1,0:T(8,128)(2,1)} %amp_hbm.1, bf16[576,128]{1,0:T(8,128)(2,1)} %forces_hbm.1, f32[576]{0:T(1024)} %freq_ref.1), custom_call_target="tpu_custom_call" | custom-call | tf_op jit(solution)/shard_map/exchange/pallas_call | solution.py:387
  90.7 5.5 %add_last.1 = f32[576,2304]{1,0:T(8,128)} custom-call(f32[576,2304]{1,0:T(8,128)} %get-tuple-element.8.grad_hbm, bf16[576,256]{1,0:T(8,128)(2,1)} %get-tuple-element.9.resid_hbm, bf16[2304,256]{1,0:T(8,128)(2,1)} %get-tuple-element.10.disp_hbm), custom_call_target="tpu_custom_call" | custom-call | tf_op jit(solution)/shard_map/add_last/pallas_call | solution.py:474

commit v5 on v4

--- a/solution.py
+++ b/solution.py
@@ -27,8 +27,8 @@
 
 
 def comm_kernel(
-    eig_hbm, fc_hbm, amp_hbm, forces_hbm, freq_ref, grad_hbm, resid_hbm, disp_hbm,
-    eig_t, eig, fc, amp, scale, part32, part16, in_opp, in_near, sum32, sum16, in_second, own32, own16, in_zl,
+    eig_hbm, fc_hbm, amp_hbm, forces_hbm, freq_hbm, grad_hbm, resid_hbm, disp_hbm,
+    freq, eig_t, eig, fc, amp, scale, part32, part16, in_opp, in_near, sum32, sum16, in_second, own32, own16, in_zl,
     disp, harm, in_core, harm32, harm16, in_zh, force_in, force_own, resid, grad,
     load_sem, col_send, col_recv, row_send, row_recv, m_send, m_recv, out_sem,
 ):
@@ -58,7 +58,8 @@
     load_eig = [pltpu.make_async_copy(eig_hbm.at[:, pl.ds(q * TILE, TILE)], eig_t.at[q], load_sem.at[13 + q]) for q in range(rows // TILE)]
     load_fc = pltpu.make_async_copy(fc_hbm, fc, load_sem.at[8])
     load_forces = [pltpu.make_async_copy(forces_hbm.at[pl.ds(q * piece, piece)], force_own.at[q], load_sem.at[9 + q]) for q in range(4)]
-    for c in load_amp[:1] + load_eig:
+    load_freq = pltpu.make_async_copy(freq_hbm, freq, load_sem.at[13 + rows // TILE])
+    for c in [load_freq] + load_amp[:1] + load_eig:
         c.start()
 
     barrier = pltpu.get_barrier_semaphore()
@@ -66,7 +67,8 @@
     for dev in peers:
         pl.semaphore_signal(barrier, inc=1, device_id=dev, device_id_type=MESH)
 
-    f = freq_ref[...].reshape(1, modes)
+    load_freq.wait()
+    f = freq[...].reshape(1, modes)
     on_diag = lax.broadcasted_iota(jnp.int32, (modes, modes), 0) == lax.broadcasted_iota(jnp.int32, (modes, modes), 1)
     f_col = jnp.sum(jnp.where(on_diag, f, 0.0), axis=1, keepdims=True)
     scale[...] = jnp.broadcast_to(1.0 / jnp.sqrt(2.0 * f_col), scale.shape)
@@ -392,9 +394,10 @@
             jax.ShapeDtypeStruct((out_rows, 2 * LANES), bf16),
             jax.ShapeDtypeStruct((rows, 2 * LANES), bf16),
         ],
-        in_specs=[anywhere] * 4 + [pl.BlockSpec(memory_space=pltpu.VMEM)],
+        in_specs=[anywhere] * 5,
         out_specs=[anywhere] * 3,
         scratch_shapes=[
+            pltpu.VMEM((modes,), f32),
             pltpu.VMEM((rows // TILE, modes, TILE), bf16),
             pltpu.VMEM((rows, modes), bf16),
             pltpu.VMEM((out_rows, rows), bf16),
@@ -420,7 +423,7 @@
             pltpu.VMEM((4, piece, LANES), bf16),
             pltpu.VMEM((PAIRS, 2, out_rows, LANES), bf16),
             pltpu.VMEM((out_rows, rows), f32),
-            dma((13 + rows // TILE,)),
+            dma((14 + rows // TILE,)),
             dma((PAIRS, 2, 19)),
             dma((PAIRS, 2, 19)),
             dma((PAIRS, 14)),

time: 96.5 us -> 95.3 us (0.988)
  Pallas kernels: 96.2 us -> 95 us
    pallas_call x1, Pallas kernels: 90.7 us -> 89.5 us  [exchange(): pl.pallas_call(comm_kernel, name='exchange', out_shape=[jax.ShapeDtypeStr...]
where the time goes in v5:
time: 95.3 us; the launch traced here: 95.2 us
  Pallas kernels  95 us (100%)
    pallas_call x1, Pallas kernels, exchange(): pl.pallas_call(comm_kernel, name='exchange', out_shape=[jax.ShapeDtypeStr...  89.5 us
    pallas_call x1, Pallas kernels, add_last(): pl.pallas_call(last_kernel, name='add_last', out_shape=jax.ShapeDtypeStru...  5.5 us

profile of v5, /device:TPU:1, one launch (start us, length us, event | category | flops | bytes accessed | tf_op | source)
XLA Modules:
  0.0 95.2 jit_solution(18376259119654392472)
XLA Ops:
  0.0 89.5 %exchange.1 = (f32[576,2304]{1,0:T(8,128)}, bf16[576,256]{1,0:T(8,128)(2,1)}, bf16[2304,256]{1,0:T(8,128)(2,1)}) custom-call(bf16[576,2304]{1,0:T(8,128)(2,1)} %bitcast.1, bf16[576,2304]{1,0:T(8,128)(2,1)} %fc_hbm.1, bf16[576,1024]{1,0:T(8,128)(2,1)} %amp_hbm.1, bf16[576,128]{1,0:T(8,128)(2,1)} %forces_hbm.1, f32[576]{0:T(1024)} %freq_hbm.1), custom_call_target="tpu_custom_call" | custom-call | tf_op jit(solution)/shard_map/exchange/pallas_call | solution.py:389
  89.5 5.5 %add_last.1 = f32[576,2304]{1,0:T(8,128)} custom-call(f32[576,2304]{1,0:T(8,128)} %get-tuple-element.8.grad_hbm, bf16[576,256]{1,0:T(8,128)(2,1)} %get-tuple-element.9.resid_hbm, bf16[2304,256]{1,0:T(8,128)(2,1)} %get-tuple-element.10.disp_hbm), custom_call_target="tpu_custom_call" | custom-call | tf_op jit(solution)/shard_map/add_last/pallas_call | solution.py:477

commit v6 on v5

--- a/solution.py
+++ b/solution.py
@@ -347,8 +347,6 @@
             grad_store(g).start()
 
     stages = [stage0, stage1, stage2, stage3, stage4, stage5, stage6, stage7, stage8, stage9, stage10, stage11, stage12]
-    for s, *which in ORDER:
-        stages[s](*which)
 
     def drain(p, carry):
         for t in range(2):
@@ -364,11 +362,21 @@
         for h in range(2):
             for d in (1, 2, 3):
                 zh_out(p, d, h).wait_send()
+        return carry
+
+    def drain_resid(p, carry):
+        for h in range(2):
+            for d in (1, 2, 3):
                 resid_spread(p, d, h, zh).wait_send()
         resid_core(p, core).wait_send()
         return carry
 
-    lax.fori_loop(0, PAIRS, drain, 0)
+    quiet = max(i for i, step in enumerate(ORDER) if step[0] == 10)
+    for i, (s, *which) in enumerate(ORDER):
+        if i == quiet:
+            lax.fori_loop(0, PAIRS, drain, 0)
+        stages[s](*which)
+    lax.fori_loop(0, PAIRS, drain_resid, 0)
     for t in range(2):
         disp_store(t).wait()
         resid_store(t).wait()

time: 95.3 us -> 95.3 us (level)
  no operation moved by 1% of the time
where the time goes in v6:
time: 95.3 us; the launch traced here: 95.2 us
  Pallas kernels  95 us (100%)
    pallas_call x1, Pallas kernels, exchange(): pl.pallas_call(comm_kernel, name='exchange', out_shape=[jax.ShapeDtypeStr...  89.5 us
    pallas_call x1, Pallas kernels, add_last(): pl.pallas_call(last_kernel, name='add_last', out_shape=jax.ShapeDtypeStru...  5.5 us

profile of v6, /device:TPU:1, one launch (start us, length us, event | category | flops | bytes accessed | tf_op | source)
XLA Modules:
  0.0 95.2 jit_solution(4341408223073623332)
XLA Ops:
  0.0 89.5 %exchange.1 = (f32[576,2304]{1,0:T(8,128)}, bf16[576,256]{1,0:T(8,128)(2,1)}, bf16[2304,256]{1,0:T(8,128)(2,1)}) custom-call(bf16[576,2304]{1,0:T(8,128)(2,1)} %bitcast.1, bf16[576,2304]{1,0:T(8,128)(2,1)} %fc_hbm.1, bf16[576,1024]{1,0:T(8,128)(2,1)} %amp_hbm.1, bf16[576,128]{1,0:T(8,128)(2,1)} %forces_hbm.1, f32[576]{0:T(1024)} %freq_hbm.1), custom_call_target="tpu_custom_call" | custom-call | tf_op jit(solution)/shard_map/exchange/pallas_call | solution.py:397
  89.5 5.5 %add_last.1 = f32[576,2304]{1,0:T(8,128)} custom-call(f32[576,2304]{1,0:T(8,128)} %get-tuple-element.8.grad_hbm, bf16[576,256]{1,0:T(8,128)(2,1)} %get-tuple-element.9.resid_hbm, bf16[2304,256]{1,0:T(8,128)(2,1)} %get-tuple-element.10.disp_hbm), custom_call_target="tpu_custom_call" | custom-call | tf_op jit(solution)/shard_map/add_last/pallas_call | solution.py:485
